TPU v7x, 128 devices: a whole 4x4x4 slice. The times are simulated.
128 devices in a mesh: org: 16 (over y, x), dst: 8 (over z, core).
Axes of the slice: x: 4, y: 4, z: 4, core: 2. Of those that a mesh axis runs over, the one named last changes fastest.
Arguments:
- counts: int32 [8, 8192, 8192], P(None, 'org', 'dst'), may hold values from 0 to 127, as said below
- block_scales: float32 [8, 64, 64], P(None, 'org', 'dst'), may hold values from 0.05 to 12.5, as said below
- anchor_factor: float32 [64, 8192], P(None, 'org'), may hold values from 0.2 to 9, as said below
- dest_factor: float32 [64, 8192], P(None, 'dst'), may hold values from 0.2 to 9, as said below
- hour_factor: float32 [8, 64], replicated, may hold values from 0.5 to 2
Outputs:
- anchor_updated: float32 [64, 8192], P(None, 'org')
- dest_updated: float32 [64, 8192], P(None, 'dst')
Inputs may be any that keep to these rules, and one draw needn't show every extreme that they name: Whole trip counts. `block_scales`: positive. `anchor_factor`: positive. `dest_factor`: positive.
All inputs are finite; a program needn't handle non-finite values.
Results may differ from a plain program's by a relative error of at most 0.0003.
Values sent between devices are 32-bit elements; how exact they have to be, the bound alone decides.
A program may use at most 128 MiB of HBM per device.

v0:
```python
import jax
import jax.numpy as jnp
from jax import lax
from jax.sharding import PartitionSpec as P

SCALE_BLOCK = 128
SWEEPS = 6


def dequantize(counts, scales):
    n_hours, row_count, col_count = counts.shape
    blocks = counts.reshape(
        n_hours, row_count // SCALE_BLOCK, SCALE_BLOCK, col_count // SCALE_BLOCK, SCALE_BLOCK
    ).astype(jnp.float32)
    values = blocks * scales[:, :, None, :, None]
    return values.reshape(n_hours, row_count, col_count).astype(jnp.bfloat16)


def anchor_products(tensor, dest_now, hour_factor):
    per_hour = jnp.einsum(
        "rj,hij->hri", dest_now.astype(jnp.bfloat16), tensor, preferred_element_type=jnp.float32
    )
    return jnp.einsum("hri,hr->ri", per_hour, hour_factor, precision=lax.Precision.HIGHEST)


def dest_products(tensor, anchor_now, hour_factor):
    per_hour = jnp.einsum(
        "ri,hij->hrj", anchor_now.astype(jnp.bfloat16), tensor, preferred_element_type=jnp.float32
    )
    return jnp.einsum("hrj,hr->rj", per_hour, hour_factor, precision=lax.Precision.HIGHEST)


def local_gram(factor):
    return jnp.dot(factor, factor.T, precision=lax.Precision.HIGHEST)


def update(factor, totals, gram_part):
    return factor * totals / jnp.dot(gram_part, factor, precision=lax.Precision.HIGHEST)


def anchor_step(anchor_now, totals, dest_now, hour_gram):
    own_gram = local_gram(dest_now)
    summed = lax.psum(totals, "dst")
    gram_part = lax.psum(own_gram, "dst") * hour_gram
    updated = update(anchor_now, summed, gram_part)
    return updated


def dest_step(dest_now, totals, anchor_now, hour_gram):
    own_gram = local_gram(anchor_now)
    summed = lax.psum(totals, "org")
    gram_part = lax.psum(own_gram, "org") * hour_gram
    updated = update(dest_now, summed, gram_part)
    return updated


def body(counts, block_scales, anchor_factor, dest_factor, hour_factor):
    tensor = dequantize(counts, block_scales)
    hour_gram = jnp.dot(hour_factor.T, hour_factor, precision=lax.Precision.HIGHEST)
    anchor_now = anchor_factor
    dest_now = dest_factor
    for sweep_index in range(SWEEPS):
        anchor_totals = anchor_products(tensor, dest_now, hour_factor)
        anchor_now = anchor_step(anchor_now, anchor_totals, dest_now, hour_gram)
        dest_totals = dest_products(tensor, anchor_now, hour_factor)
        dest_now = dest_step(dest_now, dest_totals, anchor_now, hour_gram)
    return (anchor_now, dest_now)


def solution(mesh):
    return jax.shard_map(
        body,
        mesh=mesh,
        in_specs=(
            P(None, "org", "dst"),
            P(None, "org", "dst"),
            P(None, "org"),
            P(None, "dst"),
            P(),
        ),
        out_specs=(P(None, "org"), P(None, "dst")),
        check_vma=False,
    )
```

profile of v0, /device:TPU:0, one launch (start us, length us, event | category | flops | bytes accessed | tf_op | source)
XLA Modules:
  0.0 1026.9 jit_solution(3049125957851498828)
XLA Ops:
  14.8 18.0 %mul.84 = f32[8,512,1024]{2,1,0:T(8,128)} reshape(f32[8,4,128,8,128]{4,3,2,1,0:T(8,128)} %mul.83) | data formatting | bytes 33554432 | tf_op jit(solution)/shard_map/mul | solution.py:15
  32.9 12.0 %multiply_convert_fusion = bf16[8,512,1024]{2,1,0:T(8,128)(2,1)S(1)} fusion(f32[8,512,1024]{2,1,0:T(8,128)} %mul.84, s32[8,512,1024]{2,1,0:T(8,128)} %param.5), kind=kLoop, calls=%fused_computation | loop fusion | flops 12582912 | bytes 41943040 | tf_op jit(solution)/shard_map/convert_element_type | solution.py:16
  53.8 27.0 %psum.169 = f32[64,64]{1,0:T(8,128)S(1)} all-reduce(f32[64,64]{1,0:T(8,128)S(1)} %fusion.60), channel_id=1, replica_groups=mesh['org'=16,'dst'=8] {'dst'}, use_global_device_ids=true, to_apply=%region_1.0 | all-reduce | flops 4096 | bytes 32768 | tf_op jit(solution)/shard_map/psum | solution.py:44
  80.8 34.5 %all-reduce.13.cloned.1.call-done = f32[64,512]{1,0:T(8,128)} async-done(((f32[64,512]{1,0:T(8,128)}), f32[64,512]{1,0:T(8,128)}) %all-reduce.13.cloned.1.call-update) | async-done | bytes 131088 | tf_op jit(solution)/shard_map/psum | solution.py:43
  125.8 74.3 %psum.171 = f32[64,64]{1,0:T(8,128)S(1)} all-reduce(f32[64,64]{1,0:T(8,128)S(1)} %fusion.62), channel_id=1, replica_groups=mesh['org'=16,'dst'=8] {'org'}, use_global_device_ids=true, to_apply=%region_3.0 | all-reduce | flops 4096 | bytes 32768 | tf_op jit(solution)/shard_map/psum | solution.py:52
  200.1 8.3 all-reduce.15.cloned.1.call-done
  218.5 24.6 %psum.173 = f32[64,64]{1,0:T(8,128)S(1)} all-reduce(f32[64,64]{1,0:T(8,128)S(1)} %fusion.63), channel_id=1, replica_groups=mesh['org'=16,'dst'=8] {'dst'}, use_global_device_ids=true, to_apply=%region_5.0 | all-reduce | flops 4096 | bytes 32768 | tf_op jit(solution)/shard_map/psum | solution.py:44
  243.0 34.1 %all-reduce.17.cloned.1.call-done = f32[64,512]{1,0:T(8,128)} async-done(((f32[64,512]{1,0:T(8,128)}), f32[64,512]{1,0:T(8,128)}) %all-reduce.17.cloned.1.call-update) | async-done | bytes 131088 | tf_op jit(solution)/shard_map/psum | solution.py:43
  287.5 74.8 %psum.175 = f32[64,64]{1,0:T(8,128)S(1)} all-reduce(f32[64,64]{1,0:T(8,128)S(1)} %fusion.64), channel_id=1, replica_groups=mesh['org'=16,'dst'=8] {'org'}, use_global_device_ids=true, to_apply=%region_7.0 | all-reduce | flops 4096 | bytes 32768 | tf_op jit(solution)/shard_map/psum | solution.py:52
  380.3 24.6 %psum.177 = f32[64,64]{1,0:T(8,128)S(1)} all-reduce(f32[64,64]{1,0:T(8,128)S(1)} %fusion.65), channel_id=1, replica_groups=mesh['org'=16,'dst'=8] {'dst'}, use_global_device_ids=true, to_apply=%region_9.0 | all-reduce | flops 4096 | bytes 32768 | tf_op jit(solution)/shard_map/psum | solution.py:44
  404.8 34.1 %all-reduce.21.cloned.1.call-done = f32[64,512]{1,0:T(8,128)} async-done(((f32[64,512]{1,0:T(8,128)}), f32[64,512]{1,0:T(8,128)}) %all-reduce.21.cloned.1.call-update) | async-done | bytes 131088 | tf_op jit(solution)/shard_map/psum | solution.py:43
  449.3 74.6 %psum.179 = f32[64,64]{1,0:T(8,128)S(1)} all-reduce(f32[64,64]{1,0:T(8,128)S(1)} %fusion.66), channel_id=1, replica_groups=mesh['org'=16,'dst'=8] {'org'}, use_global_device_ids=true, to_apply=%region_11.0 | all-reduce | flops 4096 | bytes 32768 | tf_op jit(solution)/shard_map/psum | solution.py:52
  523.9 8.1 all-reduce.23.cloned.1.call-done
  542.1 24.6 %psum.181 = f32[64,64]{1,0:T(8,128)S(1)} all-reduce(f32[64,64]{1,0:T(8,128)S(1)} %fusion.67), channel_id=1, replica_groups=mesh['org'=16,'dst'=8] {'dst'}, use_global_device_ids=true, to_apply=%region_13.0 | all-reduce | flops 4096 | bytes 32768 | tf_op jit(solution)/shard_map/psum | solution.py:44
  566.7 34.1 %all-reduce.25.cloned.1.call-done = f32[64,512]{1,0:T(8,128)} async-done(((f32[64,512]{1,0:T(8,128)}), f32[64,512]{1,0:T(8,128)}) %all-reduce.25.cloned.1.call-update) | async-done | bytes 131088 | tf_op jit(solution)/shard_map/psum | solution.py:43
  611.1 74.6 %psum.183 = f32[64,64]{1,0:T(8,128)S(1)} all-reduce(f32[64,64]{1,0:T(8,128)S(1)} %fusion.68), channel_id=1, replica_groups=mesh['org'=16,'dst'=8] {'org'}, use_global_device_ids=true, to_apply=%region_15.0 | all-reduce | flops 4096 | bytes 32768 | tf_op jit(solution)/shard_map/psum | solution.py:52
  685.7 8.1 all-reduce.27.cloned.1.call-done
  703.9 24.6 %psum.185 = f32[64,64]{1,0:T(8,128)S(1)} all-reduce(f32[64,64]{1,0:T(8,128)S(1)} %fusion.69), channel_id=1, replica_groups=mesh['org'=16,'dst'=8] {'dst'}, use_global_device_ids=true, to_apply=%region_17.0 | all-reduce | flops 4096 | bytes 32768 | tf_op jit(solution)/shard_map/psum | solution.py:44
  728.5 34.1 %all-reduce.29.cloned.1.call-done = f32[64,512]{1,0:T(8,128)} async-done(((f32[64,512]{1,0:T(8,128)}), f32[64,512]{1,0:T(8,128)}) %all-reduce.29.cloned.1.call-update) | async-done | bytes 131088 | tf_op jit(solution)/shard_map/psum | solution.py:43
  772.9 74.6 %psum.187 = f32[64,64]{1,0:T(8,128)S(1)} all-reduce(f32[64,64]{1,0:T(8,128)S(1)} %fusion.70), channel_id=1, replica_groups=mesh['org'=16,'dst'=8] {'org'}, use_global_device_ids=true, to_apply=%region_19.0 | all-reduce | flops 4096 | bytes 32768 | tf_op jit(solution)/shard_map/psum | solution.py:52
  865.8 24.6 %psum.189 = f32[64,64]{1,0:T(8,128)S(1)} all-reduce(f32[64,64]{1,0:T(8,128)S(1)} %fusion.71), channel_id=1, replica_groups=mesh['org'=16,'dst'=8] {'dst'}, use_global_device_ids=true, to_apply=%region_21.0 | all-reduce | flops 4096 | bytes 32768 | tf_op jit(solution)/shard_map/psum | solution.py:44
  890.3 34.1 %all-reduce.33.cloned.1.call-done = f32[64,512]{1,0:T(8,128)} async-done(((f32[64,512]{1,0:T(8,128)}), f32[64,512]{1,0:T(8,128)}) %all-reduce.33.cloned.1.call-update) | async-done | bytes 131088 | tf_op jit(solution)/shard_map/psum | solution.py:43
  934.8 74.4 %psum.191 = f32[64,64]{1,0:T(8,128)S(1)} all-reduce(f32[64,64]{1,0:T(8,128)S(1)} %fusion.72), channel_id=1, replica_groups=mesh['org'=16,'dst'=8] {'org'}, use_global_device_ids=true, to_apply=%region_23.0 | all-reduce | flops 4096 | bytes 32768 | tf_op jit(solution)/shard_map/psum | solution.py:52
  1009.2 8.3 all-reduce.35.cloned.1.call-done
  (99 shorter events, 147.0 us)
Async XLA Ops:
  7.2 108.1 %all-reduce.13.cloned.1.call-start = ((), (), s32[]{:S(2)}) async-start(), calls=%async_computation | async-start | bytes 262144 | tf_op jit(solution)/shard_map/psum | solution.py:43
  14.8 18.0 %copy-start.3 = (f32[8,64]{1,0:T(8,128)S(1)}, f32[8,64]{1,0:T(8,128)}, u32[]{:S(2)}) copy-start(f32[8,64]{1,0:T(8,128)} %param.9) | copy-start | bytes 6148
  32.9 15.3 %copy-start.1 = (f32[64,1024]{1,0:T(8,128)S(1)}, f32[64,1024]{1,0:T(8,128)}, u32[]{:S(2)}) copy-start(f32[64,1024]{1,0:T(8,128)} %param.8) | copy-start | bytes 786436
  44.9 3.2 copy-start
  48.2 67.1 %copy-start.4 = (f32[64,512]{1,0:T(8,128)S(1)}, f32[64,512]{1,0:T(8,128)}, u32[]{:S(2)}) copy-start(f32[64,512]{1,0:T(8,128)} %param.7) | copy-start | bytes 393220
  53.2 155.2 %all-reduce.15.cloned.1.call-start = ((), (), s32[]{:S(2)}) async-start(), calls=%async_computation.1 | async-start | bytes 524288 | tf_op jit(solution)/shard_map/psum | solution.py:51
  125.3 151.8 %all-reduce.17.cloned.1.call-start = ((), (), s32[]{:S(2)}) async-start(), calls=%async_computation.2 | async-start | bytes 262144 | tf_op jit(solution)/shard_map/psum | solution.py:43
  218.1 152.1 %all-reduce.19.cloned.1.call-start = ((), (), s32[]{:S(2)}) async-start(), calls=%async_computation.3 | async-start | bytes 524288 | tf_op jit(solution)/shard_map/psum | solution.py:51
  287.2 151.8 %all-reduce.21.cloned.1.call-start = ((), (), s32[]{:S(2)}) async-start(), calls=%async_computation.4 | async-start | bytes 262144 | tf_op jit(solution)/shard_map/psum | solution.py:43
  379.9 152.1 %all-reduce.23.cloned.1.call-start = ((), (), s32[]{:S(2)}) async-start(), calls=%async_computation.5 | async-start | bytes 524288 | tf_op jit(solution)/shard_map/psum | solution.py:51
  449.0 151.8 %all-reduce.25.cloned.1.call-start = ((), (), s32[]{:S(2)}) async-start(), calls=%async_computation.6 | async-start | bytes 262144 | tf_op jit(solution)/shard_map/psum | solution.py:43
  541.7 152.1 %all-reduce.27.cloned.1.call-start = ((), (), s32[]{:S(2)}) async-start(), calls=%async_computation.7 | async-start | bytes 524288 | tf_op jit(solution)/shard_map/psum | solution.py:51
  610.8 151.8 %all-reduce.29.cloned.1.call-start = ((), (), s32[]{:S(2)}) async-start(), calls=%async_computation.8 | async-start | bytes 262144 | tf_op jit(solution)/shard_map/psum | solution.py:43
  703.5 152.2 %all-reduce.31.cloned.1.call-start = ((), (), s32[]{:S(2)}) async-start(), calls=%async_computation.9 | async-start | bytes 524288 | tf_op jit(solution)/shard_map/psum | solution.py:51
  772.6 151.8 %all-reduce.33.cloned.1.call-start = ((), (), s32[]{:S(2)}) async-start(), calls=%async_computation.10 | async-start | bytes 262144 | tf_op jit(solution)/shard_map/psum | solution.py:43
  865.4 152.2 %all-reduce.35.cloned.1.call-start = ((), (), s32[]{:S(2)}) async-start(), calls=%async_computation.11 | async-start | bytes 524288 | tf_op jit(solution)/shard_map/psum | solution.py:51
  925.6 94.0 %copy-start.2 = (f32[64,512]{1,0:T(8,128)}, f32[64,512]{1,0:T(8,128)S(1)}, u32[]{:S(2)}) copy-start(f32[64,512]{1,0:T(8,128)S(1)} %convolution_divide_fusion.6) | copy-start | bytes 393220
Sparse Core Ops, SparseCore 0:
  53.3 61.9 all-reduce.12
  125.4 82.8 all-reduce.14
  218.2 58.9 all-reduce.16
  287.3 82.8 all-reduce.18
  380.0 58.9 all-reduce.20
  449.1 82.8 all-reduce.22
  541.8 58.9 all-reduce.24
  610.9 82.8 all-reduce.26
  703.6 58.9 all-reduce.28
  772.7 82.8 all-reduce.30
  865.5 58.9 all-reduce.32
  934.6 82.8 all-reduce.34
where the time goes:
time: 1040 us; the launch traced here: 1030 us
  blocking collectives  597 us (57%)
  waiting for transfers between devices  254 us (24%)
  matrix products  111 us (11%)
  local copies, waits for them, and re-layouts  37.4 us (4%)
  between operations  14.9 us (1%)
  other arithmetic  12 us (1%)
    psum x6, blocking collectives, dest_step(): gram_part = lax.psum(own_gram, 'org') * hour_gram  447 us
    psum x6, waiting for transfers between devices, anchor_step(): summed = lax.psum(totals, 'dst')  205 us
    psum x6, blocking collectives, anchor_step(): gram_part = lax.psum(own_gram, 'dst') * hour_gram  150 us
    psum x6, waiting for transfers between devices, dest_step(): summed = lax.psum(totals, 'org')  48.8 us
    dot_general x6, matrix products, anchor_products(): jnp.einsum('rj,hij->hri', dest_now.astype(jnp.bfloat16), tensor, preferre...  32.8 us
    dot_general x6, matrix products, dest_products(): jnp.einsum('ri,hij->hrj', anchor_now.astype(jnp.bfloat16), tensor, prefer...  29.7 us
    mul x2, local copies, waits for them, and re-layouts, dequantize(): values = blocks * scales[:, :, None, :, None]  25.6 us
  transfers between devices with their start and end apart: 12, of which 12 were waited for; matrix products, arithmetic and copies ran while one was open for 0% of the time, Pallas kernels for 0%

commit v1 on v0

v1 whole, which is shorter than its diff:
```python
import jax
import jax.numpy as jnp
from jax import lax
from jax.experimental import pallas as pl
from jax.experimental.pallas import tpu as pltpu
from jax.sharding import PartitionSpec as P

RANK = 64
HOURS = 8
SWEEPS = 6
WIDE = 256
SLOTS = 4
MESH = pl.DeviceIdType.MESH
HIGHEST = lax.Precision.HIGHEST
F32 = jnp.float32
BF16 = jnp.bfloat16
FAR = (2, 1, 3, 0)
NEAR = (0, 1, 3, 2)
OFFSETS = sorted(
    [(dy, dx) for dy in range(4) for dx in range(4) if (dy, dx) != (0, 0)],
    key=lambda o: -(min(o[0], 4 - o[0]) + min(o[1], 4 - o[1])),
)


def flip(offset):
    return (4 - offset) % 4


def gram(left, right):
    return lax.dot_general(
        left, right, (((1,), (1,)), ((), ())), precision=HIGHEST, preferred_element_type=F32
    )


def kernel(
    counts_ref, scales_ref, anchor_ref, dest_ref, hour_ref,
    anchor_out, dest_out,
    tensor, tensor_t, stage, weights_a, weights_b, hours_wide, hour_gram,
    anchor_own, anchor_sib, dest, dest_own, sib_send, sib_recv, slabs,
    partial, partial_mine, parts, gram_send, gram_parts, kept,
    stage_sem, in_sem, sib_sems, half_sems, slab_send, slab_recv, part_send, part_recv,
    gsend, grecv, block_send, block_recv,
):
    o = lax.axis_index("org")
    d = lax.axis_index("dst")
    y, x = o // 4, lax.rem(o, 4)
    z, c = d // 2, lax.rem(d, 2)

    def org_peer(dy, dx):
        return (lax.rem(y + dy, 4) * 4 + lax.rem(x + dx, 4), d)

    def z_peer(dz):
        return (o, lax.rem(z + dz, 4) * 2 + c)

    sibling = (o, z * 2 + 1 - c)

    def rows16(index):
        return pl.ds(pl.multiple_of(index * 16, 16), 16)

    def rows8(index):
        return pl.ds(pl.multiple_of(index * 8, 8), 8)

    def stage_copy(step):
        hour, half = step // 2, lax.rem(step, 2)
        slot = lax.rem(step, SLOTS)
        return pltpu.make_async_copy(
            counts_ref.at[hour, pl.ds(pl.multiple_of(half * WIDE, WIDE), WIDE), :],
            stage.at[slot],
            stage_sem.at[slot],
        )

    for step in range(SLOTS):
        stage_copy(step).start()

    barrier = pltpu.get_barrier_semaphore()
    for dy, dx in OFFSETS:
        pl.semaphore_signal(barrier, inc=1, device_id=org_peer(dy, dx), device_id_type=MESH)
    for dz in (1, 2, 3):
        pl.semaphore_signal(barrier, inc=1, device_id=z_peer(dz), device_id_type=MESH)
    pl.semaphore_signal(barrier, inc=1, device_id=sibling, device_id_type=MESH)

    own_columns = pl.ds(pl.multiple_of(c * WIDE, WIDE), WIDE)
    first = [pltpu.make_async_copy(anchor_ref.at[:, own_columns], anchor_own, in_sem.at[0])]
    for chunk in range(4):
        first.append(
            pltpu.make_async_copy(
                dest_ref.at[:, pl.ds(chunk * WIDE, WIDE)], dest.at[chunk], in_sem.at[1 + chunk]
            )
        )
    for copy in first:
        copy.start()

    total = None
    for hour in range(HOURS):
        wide = jnp.broadcast_to(hour_ref[hour : hour + 1, :], (128, RANK)).T
        hours_wide[hour, :, 0:128] = wide
        hours_wide[hour, :, 128:256] = wide
        term = wide[:, 0:RANK] * hour_ref[hour : hour + 1, :]
        total = term if total is None else total + term
    hour_gram[...] = total

    def load(step, carry):
        hour, half = step // 2, lax.rem(step, 2)
        slot = lax.rem(step, SLOTS)
        stage_copy(step).wait()
        base = hour * WIDE
        for ib in range(2):
            for jb in range(8):
                scale = scales_ref[hour, half * 2 + ib, jb]
                block = stage[slot, ib * 128 : ib * 128 + 128, jb * 128 : jb * 128 + 128]
                values = (block.astype(F32) * scale).astype(BF16)
                row = pl.ds(pl.multiple_of(base + ib * 128, 128), 128)
                tensor[jb // 2, half, row, (jb % 2) * 128 : (jb % 2) * 128 + 128] = values
                row = pl.ds(pl.multiple_of(base + (jb % 2) * 128, 128), 128)
                tensor_t[half, jb // 2, row, ib * 128 : ib * 128 + 128] = values.T

        @pl.when(step + SLOTS < 2 * HOURS)
        def _():
            stage_copy(step + SLOTS).start()

        return carry

    lax.fori_loop(0, 2 * HOURS, load, 0)
    for copy in first:
        copy.wait()
    pl.semaphore_wait(barrier, 19)

    def spread(factor, weights):
        low = factor.astype(BF16).astype(F32)
        for hour in range(HOURS):
            scaled = low * hours_wide[hour]
            high = scaled.astype(BF16)
            rest = (scaled - high.astype(F32)).astype(BF16)
            weights[0:RANK, hour * WIDE : hour * WIDE + WIDE] = high
            weights[RANK : 2 * RANK, hour * WIDE : hour * WIDE + WIDE] = rest

    def fold(sums):
        return sums[0:RANK] + sums[RANK : 2 * RANK]

    def block_copy(dy, dx):
        where = dest.at[y, rows16(x)]
        return pltpu.make_async_remote_copy(
            where, where, block_send.at[dy * 4 + dx], block_recv.at[flip(dy) * 4 + flip(dx)],
            device_id=org_peer(dy, dx), device_id_type=MESH,
        )

    def block_arrival(dy, dx):
        where = dest.at[lax.rem(y + dy, 4), rows16(lax.rem(x + dx, 4))]
        return pltpu.make_async_remote_copy(
            where, where, block_send.at[dy * 4 + dx], block_recv.at[dy * 4 + dx],
            device_id=org_peer(dy, dx), device_id_type=MESH,
        )

    def part_copy(dy, dx):
        return pltpu.make_async_remote_copy(
            partial.at[dy, rows16(lax.rem(x + dx, 4))], parts.at[flip(dy) * 4 + flip(dx)],
            part_send.at[dy * 4 + dx], part_recv.at[flip(dy) * 4 + flip(dx)],
            device_id=org_peer(dy, dx), device_id_type=MESH,
        )

    def part_arrival(dy, dx):
        return pltpu.make_async_remote_copy(
            partial.at[dy, rows16(lax.rem(x + dx, 4))], parts.at[dy * 4 + dx],
            part_send.at[dy * 4 + dx], part_recv.at[dy * 4 + dx],
            device_id=org_peer(dy, dx), device_id_type=MESH,
        )

    def gram_copy(dy, dx):
        return pltpu.make_async_remote_copy(
            gram_send.at[rows8(lax.rem(x + dx, 4))], gram_parts.at[flip(dy) * 4 + flip(dx)],
            gsend.at[dy * 4 + dx], grecv.at[flip(dy) * 4 + flip(dx)],
            device_id=org_peer(dy, dx), device_id_type=MESH,
        )

    def gram_arrival(dy, dx):
        return pltpu.make_async_remote_copy(
            gram_send.at[rows8(lax.rem(x + dx, 4))], gram_parts.at[dy * 4 + dx],
            gsend.at[dy * 4 + dx], grecv.at[dy * 4 + dx],
            device_id=org_peer(dy, dx), device_id_type=MESH,
        )

    sib_copy = pltpu.make_async_remote_copy(
        sib_send, sib_recv, sib_sems.at[0], sib_sems.at[1], device_id=sibling, device_id_type=MESH
    )
    half_copy = pltpu.make_async_remote_copy(
        anchor_own, anchor_sib, half_sems.at[0], half_sems.at[1],
        device_id=sibling, device_id_type=MESH,
    )

    def sweep(index, carry):
        parity = lax.rem(index, 2)

        dest_gram = None
        for k, dy in enumerate(NEAR):
            chunk = lax.rem(y + dy, 4)

            @pl.when(index > 0)
            def _():
                for dx in NEAR:
                    if (dy, dx) != (0, 0):
                        block_arrival(dy, dx).wait_recv()

            values = dest[chunk]
            if dy == 0:
                dest_own[...] = values
            spread(values, weights_b)
            term = gram(values, values)
            dest_gram = term if dest_gram is None else dest_gram + term
            if k < 3:
                for half in range(2):
                    sums = jnp.dot(
                        weights_b[...], tensor_t[half, chunk], preferred_element_type=F32
                    )
                    if k == 0:
                        kept[half] = sums
                    else:
                        kept[half] += sums
            else:
                packed = jnp.concatenate(
                    [dest_gram[16 * q : 16 * q + 16] for q in range(4)], axis=1
                )
                sums = jnp.dot(
                    weights_b[...], tensor_t[1 - c, chunk], preferred_element_type=F32
                )
                sib_send[0:RANK] = fold(kept[1 - c] + sums)
                sib_send[RANK : RANK + 16] = packed
                sib_copy.start()
                sums = jnp.dot(weights_b[...], tensor_t[c, chunk], preferred_element_type=F32)
                mine = fold(kept[c] + sums)

        sib_copy.wait_recv()
        slabs[parity, z, 0:RANK] = mine + sib_recv[0:RANK]
        slabs[parity, z, RANK : RANK + 16] = packed + sib_recv[RANK : RANK + 16]

        def slab_copy(dz):
            return pltpu.make_async_remote_copy(
                slabs.at[parity, z], slabs.at[parity, z],
                slab_send.at[dz], slab_recv.at[parity, flip(dz)],
                device_id=z_peer(dz), device_id_type=MESH,
            )

        def slab_arrival(dz):
            where = slabs.at[parity, lax.rem(z + dz, 4)]
            return pltpu.make_async_remote_copy(
                where, where, slab_send.at[dz], slab_recv.at[parity, dz],
                device_id=z_peer(dz), device_id_type=MESH,
            )

        for dz in (2, 1, 3):
            slab_copy(dz).start()
        sib_copy.wait_send()
        for dz in (1, 3, 2):
            slab_arrival(dz).wait_recv()
        summed = slabs[parity, 0] + slabs[parity, 1] + slabs[parity, 2] + slabs[parity, 3]
        square = jnp.concatenate(
            [summed[RANK : RANK + 16, 64 * q : 64 * q + 64] for q in range(4)], axis=0
        )
        below = jnp.dot(
            square * hour_gram[...], anchor_own[...], precision=HIGHEST, preferred_element_type=F32
        )
        anchor_own[...] = anchor_own[...] * summed[0:RANK] / below
        half_copy.start()
        for dz in (1, 2, 3):
            slab_copy(dz).wait_send()

        mine = anchor_own[...]
        spread(mine, weights_a.at[0])
        anchor_gram = gram(mine, mine)
        for dy in FAR:
            kept[dy] = jnp.dot(
                weights_a[0], tensor[lax.rem(y + dy, 4), c], preferred_element_type=F32
            )
        half_copy.wait()
        other = anchor_sib[...]
        spread(other, weights_a.at[1])
        anchor_gram = anchor_gram + gram(other, other)
        for q in range(4):
            gram_send[8 * q : 8 * q + 8, 0:64] = anchor_gram[16 * q : 16 * q + 8]
            gram_send[8 * q : 8 * q + 8, 64:128] = anchor_gram[16 * q + 8 : 16 * q + 16]
        for dy, dx in OFFSETS:
            gram_copy(dy, dx).start()
        for dy in FAR:
            sums = kept[dy] + jnp.dot(
                weights_a[1], tensor[lax.rem(y + dy, 4), 1 - c], preferred_element_type=F32
            )
            partial[dy] = fold(sums)
            for dx in FAR:
                if (dy, dx) != (0, 0):
                    part_copy(dy, dx).start()

        square = gram_send[rows8(x)]
        for dy, dx in OFFSETS:
            gram_arrival(dy, dx).wait_recv()
            square = square + gram_parts[dy * 4 + dx]
        square = jnp.concatenate([square[:, 0:64], square[:, 64:128]], axis=0)
        below = jnp.dot(
            square * hour_gram[rows16(x)], dest_own[...],
            precision=HIGHEST, preferred_element_type=F32,
        )
        ratio = dest_own[rows16(x)] / below
        summed = partial[0, rows16(x)]
        for dy, dx in reversed(OFFSETS):
            part_arrival(dy, dx).wait_recv()
            summed = summed + parts[dy * 4 + dx]
        dest[y, rows16(x)] = ratio * summed
        for dy, dx in OFFSETS:
            block_copy(dy, dx).start()
        for dy, dx in OFFSETS:
            gram_copy(dy, dx).wait_send()
            part_copy(dy, dx).wait_send()
            block_copy(dy, dx).wait_send()
        return carry

    lax.fori_loop(0, SWEEPS, sweep, 0)

    anchor_out[:, own_columns] = anchor_own[...]
    anchor_out[:, pl.ds(pl.multiple_of((1 - c) * WIDE, WIDE), WIDE)] = anchor_sib[...]
    for dy, dx in reversed(OFFSETS):
        block_arrival(dy, dx).wait_recv()
    for chunk in range(4):
        dest_out[:, chunk * WIDE : chunk * WIDE + WIDE] = dest[chunk]


def body(counts, block_scales, anchor_factor, dest_factor, hour_factor):
    hbm = pl.BlockSpec(memory_space=pltpu.HBM)
    vmem = pl.BlockSpec(memory_space=pltpu.VMEM)
    dma = pltpu.SemaphoreType.DMA
    columns = dest_factor.shape[1]
    rows = anchor_factor.shape[1]
    return pl.pallas_call(
        kernel,
        out_shape=(
            jax.ShapeDtypeStruct((RANK, rows), F32),
            jax.ShapeDtypeStruct((RANK, columns), F32),
        ),
        in_specs=[hbm, pl.BlockSpec(memory_space=pltpu.SMEM), hbm, hbm, vmem],
        out_specs=(vmem, vmem),
        scratch_shapes=[
            pltpu.VMEM((4, 2, HOURS * WIDE, WIDE), BF16),
            pltpu.VMEM((2, 4, HOURS * WIDE, WIDE), BF16),
            pltpu.VMEM((SLOTS, WIDE, 4 * WIDE), jnp.int32),
            pltpu.VMEM((2, 2 * RANK, HOURS * WIDE), BF16),
            pltpu.VMEM((2 * RANK, HOURS * WIDE), BF16),
            pltpu.VMEM((HOURS, RANK, WIDE), F32),
            pltpu.VMEM((RANK, RANK), F32),
            pltpu.VMEM((RANK, WIDE), F32),
            pltpu.VMEM((RANK, WIDE), F32),
            pltpu.VMEM((4, RANK, WIDE), F32),
            pltpu.VMEM((RANK, WIDE), F32),
            pltpu.VMEM((RANK + 16, WIDE), F32),
            pltpu.VMEM((RANK + 16, WIDE), F32),
            pltpu.VMEM((2, 4, RANK + 16, WIDE), F32),
            pltpu.VMEM((4, RANK, WIDE), F32),
            pltpu.VMEM((8, 128), F32),
            pltpu.VMEM((16, 16, WIDE), F32),
            pltpu.VMEM((32, 128), F32),
            pltpu.VMEM((16, 8, 128), F32),
            pltpu.VMEM((4, 2 * RANK, WIDE), F32),
            dma((SLOTS,)),
            dma((5,)),
            dma((2,)),
            dma((2,)),
            dma((4,)),
            dma((2, 4)),
            dma((16,)),
            dma((16,)),
            dma((16,)),
            dma((16,)),
            dma((16,)),
            dma((16,)),
        ],
        compiler_params=pltpu.CompilerParams(
            collective_id=0, has_side_effects=True, vmem_limit_bytes=48 * 1024 * 1024
        ),
        name="sweeps",
    )(counts, block_scales, anchor_factor, dest_factor, hour_factor)


def solution(mesh):
    return jax.shard_map(
        body,
        mesh=mesh,
        in_specs=(
            P(None, "org", "dst"),
            P(None, "org", "dst"),
            P(None, "org"),
            P(None, "dst"),
            P(),
        ),
        out_specs=(P(None, "org"), P(None, "dst")),
        check_vma=False,
    )
```

time: 1040 us -> 155 us (0.15); the launches traced: 1030 us -> 155 us
  blocking collectives: 597 us -> 0 us
  waiting for transfers between devices: 254 us -> 0 us
  Pallas kernels: 0 us -> 149 us
  matrix products: 111 us -> 0 us
  local copies, waits for them, and re-layouts: 37.4 us -> 4.61 us
  between operations: 14.9 us -> 0.65 us
  other arithmetic: 12 us -> 0 us
    psum x12 -> x0, blocking collectives: 597 us -> none  [the longest x6 447 us: dest_step(): gram_part = lax.psum(own_gram, 'org') * hour_gram]
    psum x12 -> x0, waiting for transfers between devices: 254 us -> none  [the longest x6 205 us: anchor_step(): summed = lax.psum(totals, 'dst')]
    pallas_call x0 -> x1, Pallas kernels: none -> 149 us  [body(): pl.pallas_call(kernel, out_shape=(jax.ShapeDtypeStruct((RANK, rows), F32)...]
    dot_general x49 -> x0, matrix products: 111 us -> none  [the longest x6 32.8 us: anchor_products(): jnp.einsum('rj,hij->hri', dest_now.astype(jnp.bfloat16), tensor, preferre...]
    mul x2 -> x0, local copies, waits for them, and re-layouts: 25.6 us -> none  [dequantize(): values = blocks * scales[:, :, None, :, None]]
    convert_element_type x1 -> x0, other arithmetic: 12 us -> none  [dequantize(): return values.reshape(n_hours, row_count, col_count).astype(jnp.bfloat16)]
  transfers between devices with their start and end apart: 12 -> 0, of which waited for: 12 -> 0; matrix products, arithmetic and copies ran while one was open for 0% -> 0% of each run, Pallas kernels for 0% -> 0%
where the time goes in v1:
time: 155 us
  Pallas kernels  149 us (96%)
  local copies, waits for them, and re-layouts  4.61 us (3%)
    pallas_call x1, Pallas kernels, body(): pl.pallas_call(kernel, out_shape=(jax.ShapeDtypeStruct((RANK, rows), F32)...  149 us
    unnamed x10, local copies, waits for them, and re-layouts  4.61 us

profile of v1, /device:TPU:0, one launch (start us, length us, event | category | flops | bytes accessed | tf_op | source)
XLA Modules:
  0.0 154.7 jit_solution(18003082401362739785)
XLA Ops:
  0.6 0.0 copy-start
  0.6 0.9 copy-done
  1.6 0.0 copy-start.1
  1.6 0.9 copy-done.1
  2.5 0.0 copy-start.2
  2.5 0.7 copy-done.2
  3.2 0.0 copy-start.3
  3.2 0.7 copy-done.3
  3.9 149.5 %sweeps.1 = (f32[64,512]{1,0:T(8,128)S(1)}, f32[64,1024]{1,0:T(8,128)S(1)}) custom-call(s32[8,512,1024]{2,1,0:T(8,128)} %counts_ref.1, f32[8,4,8]{2,1,0:T(4,128)S(1)} %copy-done.2, f32[64,512]{1,0:T(8,128)S(1)} %copy-done.1, f32[64,1024]{1,0:T(8,128)S(1)} %copy-done, f32[8,64]{1,0:T(8,128)S(1)} %copy-done.3), custom_call_target="tpu_custom_call" | custom-call | tf_op jit(solution)/shard_map/sweeps/pallas_call | solution.py:330
  153.4 0.7 copy.9
  154.0 0.7 copy.10
Async XLA Ops:
  0.6 1.0 copy-start
  1.6 0.9 copy-start.1
  2.5 0.7 copy-start.2
  3.2 0.7 copy-start.3

commit v2 on v1

v2 whole, which is shorter than its diff:
```python
import jax
import jax.numpy as jnp
from jax import lax
from jax.experimental import pallas as pl
from jax.experimental.pallas import tpu as pltpu
from jax.sharding import PartitionSpec as P

RANK = 64
HOURS = 8
SWEEPS = 6
WIDE = 256
SLOTS = 4
MESH = pl.DeviceIdType.MESH
HIGHEST = lax.Precision.HIGHEST
F32 = jnp.float32
BF16 = jnp.bfloat16
FAR = (2, 1, 3, 0)
NEAR = (0, 1, 3, 2)
OFFSETS = sorted(
    [(dy, dx) for dy in range(4) for dx in range(4) if (dy, dx) != (0, 0)],
    key=lambda o: -(min(o[0], 4 - o[0]) + min(o[1], 4 - o[1])),
)


def flip(offset):
    return (4 - offset) % 4


def gram(left, right):
    return lax.dot_general(
        left, right, (((1,), (1,)), ((), ())), precision=HIGHEST, preferred_element_type=F32
    )


def kernel(
    counts_ref, scales_ref, anchor_ref, dest_ref, hour_ref,
    anchor_out, dest_out,
    tensor, tensor_t, stage, scales, hours, weights_a, weights_b, hours_wide, hour_gram,
    anchor_own, anchor_sib, dest, dest_own, mine, sib_send, sib_recv, sib_gram, sib_gram_recv,
    org_gram, org_gram_recv,
    slabs, gram_slabs, partial, parts, gram_send, gram_parts, kept, square_sum,
    stage_sem, in_sem, sib_sems, half_sems, slab_send, slab_recv, gslab_send, gslab_recv,
    part_send, part_recv, gsend, grecv, block_send, block_recv,
):
    o = lax.axis_index("org")
    d = lax.axis_index("dst")
    y, x = o // 4, lax.rem(o, 4)
    z, c = d // 2, lax.rem(d, 2)

    def org_peer(dy, dx):
        return (lax.rem(y + dy, 4) * 4 + lax.rem(x + dx, 4), d)

    def z_peer(dz):
        return (o, lax.rem(z + dz, 4) * 2 + c)

    sibling = (o, z * 2 + 1 - c)

    def rows16(index):
        return pl.ds(pl.multiple_of(index * 16, 16), 16)

    def rows8(index):
        return pl.ds(pl.multiple_of(index * 8, 8), 8)

    def rows_of(hour):
        return pl.ds(pl.multiple_of(hour * WIDE, WIDE), WIDE)

    def stage_copy(step):
        hour, half = lax.rem(step, 8), lax.rem(1 - c + step // 8, 2)
        slot = lax.rem(step, SLOTS)
        return pltpu.make_async_copy(
            counts_ref.at[hour, rows_of(half), :], stage.at[slot], stage_sem.at[slot]
        )

    own_columns = rows_of(c)
    first = [
        pltpu.make_async_copy(scales_ref, scales, in_sem.at[0]),
        pltpu.make_async_copy(hour_ref, hours, in_sem.at[1]),
        pltpu.make_async_copy(anchor_ref.at[:, own_columns], anchor_own, in_sem.at[2]),
    ]
    for chunk in range(4):
        first.append(
            pltpu.make_async_copy(
                dest_ref.at[:, pl.ds(chunk * WIDE, WIDE)], dest.at[chunk], in_sem.at[3 + chunk]
            )
        )
    for copy in first:
        copy.start()
    for step in range(SLOTS):
        stage_copy(step).start()

    barrier = pltpu.get_barrier_semaphore()
    for dy, dx in OFFSETS:
        pl.semaphore_signal(barrier, inc=1, device_id=org_peer(dy, dx), device_id_type=MESH)
    for dz in (1, 2, 3):
        pl.semaphore_signal(barrier, inc=1, device_id=z_peer(dz), device_id_type=MESH)
    pl.semaphore_signal(barrier, inc=1, device_id=sibling, device_id_type=MESH)

    for copy in first:
        copy.wait()

    total = None
    for hour in range(HOURS):
        wide = jnp.broadcast_to(hours[hour : hour + 1, :], (128, RANK)).T
        hours_wide[hour, :, 0:128] = wide
        hours_wide[hour, :, 128:256] = wide
        term = wide[:, 0:RANK] * hours[hour : hour + 1, :]
        total = term if total is None else total + term
    hour_gram[...] = total

    def spread(factor, weights):
        low = factor.astype(BF16).astype(F32)
        for hour in range(HOURS):
            scaled = low * hours_wide[hour]
            high = scaled.astype(BF16)
            rest = (scaled - high.astype(F32)).astype(BF16)
            weights[0:RANK, hour * WIDE : hour * WIDE + WIDE] = high
            weights[RANK : 2 * RANK, hour * WIDE : hour * WIDE + WIDE] = rest

    def fold(sums):
        return sums[0:RANK] + sums[RANK : 2 * RANK]

    def pack(square):
        return jnp.concatenate([square[16 * q : 16 * q + 16] for q in range(4)], axis=1)

    dest_gram = None
    for chunk in range(4):
        spread(dest[chunk], weights_b.at[chunk])
        term = gram(dest[chunk], dest[chunk])
        dest_gram = term if dest_gram is None else dest_gram + term
    dest_own[...] = dest[y]
    gram_slabs[0, z] = pack(dest_gram)
    kept[...] = jnp.zeros_like(kept)

    sib_copy = pltpu.make_async_remote_copy(
        sib_send, sib_recv, sib_sems.at[0], sib_sems.at[1], device_id=sibling, device_id_type=MESH
    )
    sib_gram_copy = pltpu.make_async_remote_copy(
        sib_gram, sib_gram_recv, sib_sems.at[2], sib_sems.at[3],
        device_id=sibling, device_id_type=MESH,
    )
    org_gram_copy = pltpu.make_async_remote_copy(
        org_gram, org_gram_recv, sib_sems.at[4], sib_sems.at[5],
        device_id=sibling, device_id_type=MESH,
    )
    half_copy = pltpu.make_async_remote_copy(
        anchor_own, anchor_sib, half_sems.at[0], half_sems.at[1],
        device_id=sibling, device_id_type=MESH,
    )

    def z_copy(slots, send, recv, parity, dz):
        return pltpu.make_async_remote_copy(
            slots.at[parity, z], slots.at[parity, z], send.at[dz], recv.at[parity, flip(dz)],
            device_id=z_peer(dz), device_id_type=MESH,
        )

    def z_arrival(slots, send, recv, parity, dz):
        where = slots.at[parity, lax.rem(z + dz, 4)]
        return pltpu.make_async_remote_copy(
            where, where, send.at[dz], recv.at[parity, dz],
            device_id=z_peer(dz), device_id_type=MESH,
        )

    slab = (slabs, slab_send, slab_recv)
    gram_slab = (gram_slabs, gslab_send, gslab_recv)

    def load(step, carry):
        hour, half = lax.rem(step, 8), lax.rem(1 - c + step // 8, 2)
        slot = lax.rem(step, SLOTS)
        stage_copy(step).wait()
        for ib in range(2):
            for jb in range(8):
                scale = scales[hour, half * 2 + ib, jb]
                block = stage[slot, ib * 128 : ib * 128 + 128, jb * 128 : jb * 128 + 128]
                values = (block.astype(F32) * scale).astype(BF16)
                row = pl.ds(pl.multiple_of(hour * WIDE + ib * 128, 128), 128)
                tensor[jb // 2, half, row, (jb % 2) * 128 : (jb % 2) * 128 + 128] = values

        @pl.when(step + SLOTS < 2 * HOURS)
        def _():
            stage_copy(step + SLOTS).start()

        sums = kept[step // 8]
        for chunk in range(4):
            sums = sums + lax.dot_general(
                weights_b[chunk, :, rows_of(hour)], tensor[chunk, half, rows_of(hour), :],
                (((1,), (1,)), ((), ())), preferred_element_type=F32,
            )
        kept[step // 8] = sums
        return carry

    lax.fori_loop(0, HOURS, load, 0)
    sib_send[...] = fold(kept[0])
    pl.semaphore_wait(barrier, 19)
    sib_copy.start()
    for dz in (2, 1, 3):
        z_copy(*gram_slab, 0, dz).start()
    lax.fori_loop(HOURS, 2 * HOURS, load, 0)
    mine[...] = fold(kept[1])

    def block_copy(dy, dx):
        where = dest.at[y, rows16(x)]
        return pltpu.make_async_remote_copy(
            where, where, block_send.at[dy * 4 + dx], block_recv.at[flip(dy) * 4 + flip(dx)],
            device_id=org_peer(dy, dx), device_id_type=MESH,
        )

    def block_arrival(dy, dx):
        where = dest.at[lax.rem(y + dy, 4), rows16(lax.rem(x + dx, 4))]
        return pltpu.make_async_remote_copy(
            where, where, block_send.at[dy * 4 + dx], block_recv.at[dy * 4 + dx],
            device_id=org_peer(dy, dx), device_id_type=MESH,
        )

    def part_copy(dy, dx):
        return pltpu.make_async_remote_copy(
            partial.at[dy, rows16(lax.rem(x + dx, 4))], parts.at[flip(dy) * 4 + flip(dx)],
            part_send.at[dy * 4 + dx], part_recv.at[flip(dy) * 4 + flip(dx)],
            device_id=org_peer(dy, dx), device_id_type=MESH,
        )

    def part_arrival(dy, dx):
        return pltpu.make_async_remote_copy(
            partial.at[dy, rows16(lax.rem(x + dx, 4))], parts.at[dy * 4 + dx],
            part_send.at[dy * 4 + dx], part_recv.at[dy * 4 + dx],
            device_id=org_peer(dy, dx), device_id_type=MESH,
        )

    def gram_copy(dy, dx):
        return pltpu.make_async_remote_copy(
            gram_send.at[rows8(lax.rem(x + dx, 4))], gram_parts.at[flip(dy) * 4 + flip(dx)],
            gsend.at[dy * 4 + dx], grecv.at[flip(dy) * 4 + flip(dx)],
            device_id=org_peer(dy, dx), device_id_type=MESH,
        )

    def gram_arrival(dy, dx):
        return pltpu.make_async_remote_copy(
            gram_send.at[rows8(lax.rem(x + dx, 4))], gram_parts.at[dy * 4 + dx],
            gsend.at[dy * 4 + dx], grecv.at[dy * 4 + dx],
            device_id=org_peer(dy, dx), device_id_type=MESH,
        )

    def sweep(index, carry):
        parity = lax.rem(index, 2)

        sib_copy.wait_recv()
        slabs[parity, z] = mine[...] + sib_recv[...]
        for dz in (2, 1, 3):
            z_copy(*slab, parity, dz).start()
        sib_copy.wait_send()

        @pl.when(index == 0)
        def _():
            def turn(step, carry):
                half, chunk = lax.rem(step, 2), lax.rem(step // 2, 4)
                hour = rows_of(step // 8)
                tensor_t[half, chunk, hour, :] = tensor[chunk, half, hour, :].T
                return carry

            lax.fori_loop(0, 8 * HOURS, turn, 0)

        for dz in (1, 3, 2):
            z_arrival(*gram_slab, parity, dz).wait_recv()
        summed = (gram_slabs[parity, 0] + gram_slabs[parity, 1]) + (
            gram_slabs[parity, 2] + gram_slabs[parity, 3]
        )
        sib_gram[...] = summed
        sib_gram_copy.start()
        for dz in (1, 2, 3):
            z_copy(*gram_slab, parity, dz).wait_send()
        sib_gram_copy.wait()
        summed = summed + sib_gram_recv[...]
        square = jnp.concatenate([summed[:, 64 * q : 64 * q + 64] for q in range(4)], axis=0)
        below = jnp.dot(
            square * hour_gram[...], anchor_own[...], precision=HIGHEST, preferred_element_type=F32
        )
        ratio = anchor_own[...] / below
        for dz in (1, 3, 2):
            z_arrival(*slab, parity, dz).wait_recv()
        summed = (slabs[parity, 0] + slabs[parity, 1]) + (slabs[parity, 2] + slabs[parity, 3])
        own = ratio * summed
        anchor_own[...] = own
        half_copy.start()

        spread(own, weights_a.at[0])
        anchor_gram = gram(own, own)
        for q in range(4):
            low, high = 8 * q, 8 * q + 8
            gram_send[low:high, 0:64] = anchor_gram[16 * q : 16 * q + 8]
            gram_send[low:high, 64:128] = anchor_gram[16 * q + 8 : 16 * q + 16]
        for dy, dx in OFFSETS:
            gram_copy(dy, dx).start()
        for dy in FAR:
            kept[dy] = jnp.dot(
                weights_a[0], tensor[lax.rem(y + dy, 4), c], preferred_element_type=F32
            )
        for dz in (1, 2, 3):
            z_copy(*slab, parity, dz).wait_send()
        half_copy.wait()
        other = anchor_sib[...]
        spread(other, weights_a.at[1])
        for dy in FAR:
            sums = kept[dy] + jnp.dot(
                weights_a[1], tensor[lax.rem(y + dy, 4), 1 - c], preferred_element_type=F32
            )
            partial[dy] = fold(sums)
            for dx in FAR:
                if (dy, dx) != (0, 0):
                    part_copy(dy, dx).start()

        square = gram_send[rows8(x)]
        for dy, dx in reversed(OFFSETS):
            gram_arrival(dy, dx).wait_recv()
            square = square + gram_parts[dy * 4 + dx]
        org_gram[...] = square
        org_gram_copy.start()
        org_gram_copy.wait()
        square = square + org_gram_recv[...]
        square = jnp.concatenate([square[:, 0:64], square[:, 64:128]], axis=0)
        below = jnp.dot(
            square * hour_gram[rows16(x)], dest_own[...],
            precision=HIGHEST, preferred_element_type=F32,
        )
        ratio = dest_own[rows16(x)] / below
        summed = partial[0, rows16(x)]
        for dy, dx in reversed(OFFSETS):
            part_arrival(dy, dx).wait_recv()
            summed = summed + parts[dy * 4 + dx]
        dest[y, rows16(x)] = ratio * summed
        for dy, dx in OFFSETS:
            block_copy(dy, dx).start()
        for dy, dx in OFFSETS:
            gram_copy(dy, dx).wait_send()
            part_copy(dy, dx).wait_send()

        for k, dy in enumerate(NEAR):
            chunk = lax.rem(y + dy, 4)
            for dx in NEAR:
                if (dy, dx) != (0, 0):
                    block_arrival(dy, dx).wait_recv()

            @pl.when(index < SWEEPS - 1)
            def _():
                values = dest[chunk]
                weights = weights_b.at[k]
                spread(values, weights)
                if dy == 0:
                    dest_own[...] = values
                if k < 3:
                    for half in range(2):
                        sums = jnp.dot(
                            weights[...], tensor_t[half, chunk], preferred_element_type=F32
                        )
                        if k == 0:
                            kept[half] = sums
                        else:
                            kept[half] += sums
                    term = gram(values, values)
                    if k == 0:
                        square_sum[...] = term
                    else:
                        square_sum[...] += term
                else:
                    sums = jnp.dot(
                        weights[...], tensor_t[1 - c, chunk], preferred_element_type=F32
                    )
                    sib_send[...] = fold(kept[1 - c] + sums)
                    sib_copy.start()
                    gram_slabs[1 - parity, z] = pack(square_sum[...] + gram(values, values))
                    for dz in (2, 1, 3):
                        z_copy(*gram_slab, 1 - parity, dz).start()
                    sums = jnp.dot(weights[...], tensor_t[c, chunk], preferred_element_type=F32)
                    mine[...] = fold(kept[c] + sums)

        for dy, dx in OFFSETS:
            block_copy(dy, dx).wait_send()
        return carry

    lax.fori_loop(0, SWEEPS, sweep, 0)

    anchor_out[:, own_columns] = anchor_own[...]
    anchor_out[:, rows_of(1 - c)] = anchor_sib[...]
    for chunk in range(4):
        dest_out[:, chunk * WIDE : chunk * WIDE + WIDE] = dest[chunk]


def body(counts, block_scales, anchor_factor, dest_factor, hour_factor):
    hbm = pl.BlockSpec(memory_space=pltpu.HBM)
    vmem = pl.BlockSpec(memory_space=pltpu.VMEM)
    dma = pltpu.SemaphoreType.DMA
    columns = dest_factor.shape[1]
    rows = anchor_factor.shape[1]
    small = [
        pltpu.with_memory_space_constraint(value, pltpu.HBM)
        for value in (block_scales, anchor_factor, dest_factor, hour_factor)
    ]
    return pl.pallas_call(
        kernel,
        out_shape=(
            jax.ShapeDtypeStruct((RANK, rows), F32),
            jax.ShapeDtypeStruct((RANK, columns), F32),
        ),
        in_specs=[hbm] * 5,
        out_specs=(vmem, vmem),
        scratch_shapes=[
            pltpu.VMEM((4, 2, HOURS * WIDE, WIDE), BF16),
            pltpu.VMEM((2, 4, HOURS * WIDE, WIDE), BF16),
            pltpu.VMEM((SLOTS, WIDE, 4 * WIDE), jnp.int32),
            pltpu.SMEM((HOURS, 4, 8), F32),
            pltpu.VMEM((HOURS, RANK), F32),
            pltpu.VMEM((2, 2 * RANK, HOURS * WIDE), BF16),
            pltpu.VMEM((4, 2 * RANK, HOURS * WIDE), BF16),
            pltpu.VMEM((HOURS, RANK, WIDE), F32),
            pltpu.VMEM((RANK, RANK), F32),
            pltpu.VMEM((RANK, WIDE), F32),
            pltpu.VMEM((RANK, WIDE), F32),
            pltpu.VMEM((4, RANK, WIDE), F32),
            pltpu.VMEM((RANK, WIDE), F32),
            pltpu.VMEM((RANK, WIDE), F32),
            pltpu.VMEM((RANK, WIDE), F32),
            pltpu.VMEM((RANK, WIDE), F32),
            pltpu.VMEM((16, WIDE), F32),
            pltpu.VMEM((16, WIDE), F32),
            pltpu.VMEM((8, 128), F32),
            pltpu.VMEM((8, 128), F32),
            pltpu.VMEM((2, 4, RANK, WIDE), F32),
            pltpu.VMEM((2, 4, 16, WIDE), F32),
            pltpu.VMEM((4, RANK, WIDE), F32),
            pltpu.VMEM((16, 16, WIDE), F32),
            pltpu.VMEM((32, 128), F32),
            pltpu.VMEM((16, 8, 128), F32),
            pltpu.VMEM((4, 2 * RANK, WIDE), F32),
            pltpu.VMEM((RANK, RANK), F32),
            dma((SLOTS,)),
            dma((7,)),
            dma((6,)),
            dma((2,)),
            dma((4,)),
            dma((2, 4)),
            dma((4,)),
            dma((2, 4)),
            dma((16,)),
            dma((16,)),
            dma((16,)),
            dma((16,)),
            dma((16,)),
            dma((16,)),
        ],
        compiler_params=pltpu.CompilerParams(
            collective_id=0, has_side_effects=True, vmem_limit_bytes=50 * 1024 * 1024
        ),
        name="sweeps",
    )(counts, *small)


def solution(mesh):
    return jax.shard_map(
        body,
        mesh=mesh,
        in_specs=(
            P(None, "org", "dst"),
            P(None, "org", "dst"),
            P(None, "org"),
            P(None, "dst"),
            P(),
        ),
        out_specs=(P(None, "org"), P(None, "dst")),
        check_vma=False,
    )
```

time: 155 us -> 141 us (0.910)
  Pallas kernels: 149 us -> 139 us
  local copies, waits for them, and re-layouts: 4.61 us -> 1.36 us
    pallas_call x1, Pallas kernels: 149 us -> 139 us  [body(): pl.pallas_call(kernel, out_shape=(jax.ShapeDtypeStruct((RANK, rows), F32)...]
    unnamed x10 -> x2, local copies, waits for them, and re-layouts: 4.61 us -> 1.36 us
where the time goes in v2:
time: 141 us
  Pallas kernels  139 us (99%)
    pallas_call x1, Pallas kernels, body(): pl.pallas_call(kernel, out_shape=(jax.ShapeDtypeStruct((RANK, rows), F32)...  139 us

profile of v2, /device:TPU:0, one launch (start us, length us, event | category | flops | bytes accessed | tf_op | source)
XLA Modules:
  0.0 141.3 jit_solution(7606492275930115207)
XLA Ops:
  0.6 139.3 %sweeps.1 = (f32[64,512]{1,0:T(8,128)S(1)}, f32[64,1024]{1,0:T(8,128)S(1)}) custom-call(s32[8,512,1024]{2,1,0:T(8,128)} %counts_ref.1, f32[8,4,8]{2,1,0:T(4,128)} %scales_ref.1, f32[64,512]{1,0:T(8,128)} %anchor_ref.1, f32[64,1024]{1,0:T(8,128)} %dest_ref.1, f32[8,64]{1,0:T(8,128)} %hour_ref.1), custom_call_target="tpu_custom_call" | custom-call | tf_op jit(solution)/shard_map/sweeps/pallas_call | solution.py:396
  140.0 0.7 copy.9
  140.6 0.7 copy.10

commit v3 on v2

--- a/solution.py
+++ b/solution.py
@@ -239,6 +239,12 @@
             device_id=org_peer(dy, dx), device_id_type=MESH,
         )
 
+    def turn(step, carry):
+        half, chunk = lax.rem(step, 2), lax.rem(step // 2, 4)
+        hour = rows_of(step // 8)
+        tensor_t[half, chunk, hour, :] = tensor[chunk, half, hour, :].T
+        return carry
+
     def sweep(index, carry):
         parity = lax.rem(index, 2)
 
@@ -250,13 +256,7 @@
 
         @pl.when(index == 0)
         def _():
-            def turn(step, carry):
-                half, chunk = lax.rem(step, 2), lax.rem(step // 2, 4)
-                hour = rows_of(step // 8)
-                tensor_t[half, chunk, hour, :] = tensor[chunk, half, hour, :].T
-                return carry
-
-            lax.fori_loop(0, 8 * HOURS, turn, 0)
+            lax.fori_loop(0, 4 * HOURS, turn, 0)
 
         for dz in (1, 3, 2):
             z_arrival(*gram_slab, parity, dz).wait_recv()
@@ -307,6 +307,10 @@
                 if (dy, dx) != (0, 0):
                     part_copy(dy, dx).start()
 
+        @pl.when(index == 0)
+        def _():
+            lax.fori_loop(4 * HOURS, 8 * HOURS, turn, 0)
+
         square = gram_send[rows8(x)]
         for dy, dx in reversed(OFFSETS):
             gram_arrival(dy, dx).wait_recv()
@@ -363,9 +367,10 @@
                     sums = jnp.dot(
                         weights[...], tensor_t[1 - c, chunk], preferred_element_type=F32
                     )
+                    square = square_sum[...] + gram(values, values)
                     sib_send[...] = fold(kept[1 - c] + sums)
                     sib_copy.start()
-                    gram_slabs[1 - parity, z] = pack(square_sum[...] + gram(values, values))
+                    gram_slabs[1 - parity, z] = pack(square)
                     for dz in (2, 1, 3):
                         z_copy(*gram_slab, 1 - parity, dz).start()
                     sums = jnp.dot(weights[...], tensor_t[c, chunk], preferred_element_type=F32)
@@ -381,6 +386,17 @@
     anchor_out[:, rows_of(1 - c)] = anchor_sib[...]
     for chunk in range(4):
         dest_out[:, chunk * WIDE : chunk * WIDE + WIDE] = dest[chunk]
+
+
+def place(anchor_ref, dest_ref, anchor_out, dest_out, sems):
+    copies = (
+        pltpu.make_async_copy(anchor_ref, anchor_out, sems.at[0]),
+        pltpu.make_async_copy(dest_ref, dest_out, sems.at[1]),
+    )
+    for copy in copies:
+        copy.start()
+    for copy in copies:
+        copy.wait()
 
 
 def body(counts, block_scales, anchor_factor, dest_factor, hour_factor):
@@ -393,7 +409,7 @@
         pltpu.with_memory_space_constraint(value, pltpu.HBM)
         for value in (block_scales, anchor_factor, dest_factor, hour_factor)
     ]
-    return pl.pallas_call(
+    anchor, dest = pl.pallas_call(
         kernel,
         out_shape=(
             jax.ShapeDtypeStruct((RANK, rows), F32),
@@ -450,6 +466,18 @@
         ),
         name="sweeps",
     )(counts, *small)
+    return pl.pallas_call(
+        place,
+        out_shape=(
+            jax.ShapeDtypeStruct((RANK, rows), F32),
+            jax.ShapeDtypeStruct((RANK, columns), F32),
+        ),
+        in_specs=[vmem, vmem],
+        out_specs=(hbm, hbm),
+        scratch_shapes=[dma((2,))],
+        compiler_params=pltpu.CompilerParams(vmem_limit_bytes=2 * 1024 * 1024),
+        name="place",
+    )(anchor, dest)
 
 
 def solution(mesh):

time: 141 us -> 138 us (0.979)
  Pallas kernels: 139 us -> 137 us
    pallas_call x1, Pallas kernels: 139 us -> 137 us  [body(): pl.pallas_call(kernel, out_shape=(jax.ShapeDtypeStruct((RANK, rows), F32)...]
where the time goes in v3:
time: 138 us
  Pallas kernels  137 us (99%)
    pallas_call x1, Pallas kernels, body(): pl.pallas_call(kernel, out_shape=(jax.ShapeDtypeStruct((RANK, rows), F32)...  137 us

profile of v3, /device:TPU:0, one launch (start us, length us, event | category | flops | bytes accessed | tf_op | source)
XLA Modules:
  0.0 138.1 jit_solution(16797055270831458352)
XLA Ops:
  0.6 136.7 %sweeps.1 = (f32[64,512]{1,0:T(8,128)S(1)}, f32[64,1024]{1,0:T(8,128)S(1)}) custom-call(s32[8,512,1024]{2,1,0:T(8,128)} %counts_ref.1, f32[8,4,8]{2,1,0:T(4,128)} %scales_ref.1, f32[64,512]{1,0:T(8,128)} %anchor_ref.1, f32[64,1024]{1,0:T(8,128)} %dest_ref.1, f32[8,64]{1,0:T(8,128)} %hour_ref.1), custom_call_target="tpu_custom_call" | custom-call | tf_op jit(solution)/shard_map/sweeps/pallas_call | solution.py:412
  137.3 0.8 place.1

commit v4 on v3

--- a/solution.py
+++ b/solution.py
@@ -281,8 +281,8 @@
         anchor_own[...] = own
         half_copy.start()
 
+        anchor_gram = gram(own, own)
         spread(own, weights_a.at[0])
-        anchor_gram = gram(own, own)
         for q in range(4):
             low, high = 8 * q, 8 * q + 8
             gram_send[low:high, 0:64] = anchor_gram[16 * q : 16 * q + 8]
@@ -330,8 +330,10 @@
             part_arrival(dy, dx).wait_recv()
             summed = summed + parts[dy * 4 + dx]
         dest[y, rows16(x)] = ratio * summed
-        for dy, dx in OFFSETS:
-            block_copy(dy, dx).start()
+        for dy in FAR:
+            for dx in FAR:
+                if (dy, dx) != (0, 0):
+                    block_copy(dy, dx).start()
         for dy, dx in OFFSETS:
             gram_copy(dy, dx).wait_send()
             part_copy(dy, dx).wait_send()

time: 138 us -> 139 us (level)
  no operation moved by 1% of the time
where the time goes in v4:
time: 139 us
  Pallas kernels  138 us (99%)
    pallas_call x1, Pallas kernels, body(): pl.pallas_call(kernel, out_shape=(jax.ShapeDtypeStruct((RANK, rows), F32)...  137 us

profile of v4, /device:TPU:0, one launch (start us, length us, event | category | flops | bytes accessed | tf_op | source)
XLA Modules:
  0.0 138.6 jit_solution(6109862663599238859)
XLA Ops:
  0.6 137.1 %sweeps.1 = (f32[64,512]{1,0:T(8,128)S(1)}, f32[64,1024]{1,0:T(8,128)S(1)}) custom-call(s32[8,512,1024]{2,1,0:T(8,128)} %counts_ref.1, f32[8,4,8]{2,1,0:T(4,128)} %scales_ref.1, f32[64,512]{1,0:T(8,128)} %anchor_ref.1, f32[64,1024]{1,0:T(8,128)} %dest_ref.1, f32[8,64]{1,0:T(8,128)} %hour_ref.1), custom_call_target="tpu_custom_call" | custom-call | tf_op jit(solution)/shard_map/sweeps/pallas_call | solution.py:414
  137.8 0.8 place.1
